TPU v7x, 256 devices: a whole 4x4x8 slice. The times are simulated.
256 devices in a mesh: row: 16 (over y, x), col: 16 (over z, core).
Axes of the slice: x: 4, y: 4, z: 8, core: 2. Of those that a mesh axis runs over, the one named last changes fastest.
Arguments:
- g0_values: bfloat16 [8192, 8192], P('row', 'col'), may hold values from -6 to 6
- g0_pattern: int32 [64, 64], P('row', 'col'), may hold values 0 or 1
- sigma_values: bfloat16 [16, 96, 128, 128], P('row', 'col'), may hold values from -0.0014648438 to 0.0014648438
- sigma_pairs: int32 [16, 96, 2], P('row', 'col'), may hold values from 0 to 63, as said below
- sigma_count: int32 [16, 16], P('row', 'col'), may hold values from 1 to 6, as said below
Outputs:
- g_full: bfloat16 [8192, 8192], P('row', 'col')
Inputs may be any that keep to these rules, and one draw needn't show every extreme that they name: `sigma_pairs`: slot pairs of the device at position (g, o) name blocks with block row in g * 4 to g * 4 + 3 and block column in o * 4 to o * 4 + 3; the pairs of one device are distinct. `sigma_count`: count of live slots, which are the first ones of a device.
All inputs are finite; a program needn't handle non-finite values. No bound on the sum of `g0_pattern` on one device may be relied on, other than what follows from the above.
Results may differ from a plain program's by a relative error of at most 0.0037.
Values may be sent and summed in bfloat16 or wider, within the bound.
A program may use at most 128 MiB of HBM per device.

v0:
```python
import jax
import jax.numpy as jnp
from jax import lax
from jax.sharding import PartitionSpec as P


def per_device(g0_values, g0_pattern, sigma_values, sigma_pairs, sigma_count):
    block_rows = g0_pattern.shape[0]
    block_cols = g0_pattern.shape[1]
    width = sigma_values.shape[-1]
    slot_total = sigma_values.shape[1]
    mask = jnp.repeat(jnp.repeat(g0_pattern, width, axis=0), width, axis=1)
    g0_tile = g0_values * mask.astype(jnp.bfloat16)
    panel = lax.all_gather(g0_tile, "col", axis=1, tiled=True)
    live = jnp.arange(slot_total, dtype=jnp.int32) < sigma_count[0, 0]
    local_k = jnp.where(live, sigma_pairs[0, :, 0] % block_rows, block_rows)
    local_j = sigma_pairs[0, :, 1] % block_cols
    dense = jnp.zeros((block_rows, width, block_cols, width), jnp.bfloat16)
    dense = dense.at[local_k, :, local_j, :].add(sigma_values[0], mode="drop")
    sigma_tile = dense.reshape(block_rows * width, block_cols * width)
    columns = panel
    left_sum = jnp.dot(
        columns,
        lax.all_gather(sigma_tile, "row", axis=0, tiled=True),
        preferred_element_type=jnp.float32,
    )
    left_tile = left_sum.astype(jnp.bfloat16)
    start_value = g0_tile.astype(jnp.float32)
    left_panel = lax.all_gather(left_tile, "col", axis=1, tiled=True)
    columns = left_panel
    result = start_value + jnp.dot(
        columns,
        lax.all_gather(g0_tile, "row", axis=0, tiled=True),
        preferred_element_type=jnp.float32,
    )
    return result.astype(jnp.bfloat16)


def solution(mesh):
    placed = (
        P("row", "col"),
        P("row", "col"),
        P("row", "col", None, None),
        P("row", "col", None),
        P("row", "col"),
    )
    return jax.shard_map(
        per_device, mesh=mesh, in_specs=placed, out_specs=P("row", "col"), check_vma=False
    )
```

profile of v0, /device:TPU:1, one launch (start us, length us, event | category | flops | bytes accessed | tf_op | source)
XLA Modules:
  0.0 299.8 jit_solution(1443495275628197058)
XLA Ops:
  6.5 0.0 all-gather.5.cloned.1.call-start
  6.5 0.7 convert_element_type.20
  7.2 0.6 broadcast_in_dim.14
  7.9 1.9 bitcast_multiply_fusion
  9.8 0.0 all-gather.5.cloned.1.call-update
  9.8 0.0 all-gather.7.cloned.1.call-start
  10.5 0.8 fusion.4
  11.3 0.1 broadcast_in_dim.15
  11.4 2.0 scatter_fusion
  13.4 0.4 copy.6
  13.8 0.9 copy.11
  14.7 0.0 all-gather.7.cloned.1.call-update
  14.7 0.0 all-gather.11.cloned.1.call-start
  14.8 0.7 all-gather.11.cloned.1.call-update
  15.5 0.0 copy-start
  15.5 0.0 all-gather.9.cloned.1.call-start
  15.5 54.6 %all-gather.5.cloned.1.call-done = bf16[512,8192]{1,0:T(8,128)(2,1)} async-done(((bf16[512,512]{1,0:T(8,128)(2,1)}), bf16[512,8192]{1,0:T(8,128)(2,1)}) %all-gather.5.cloned.1.call-update) | async-done | bytes 8388624 | tf_op jit(solution)/shard_map/all_gather | solution.py:14
  70.1 76.4 %all-gather.7.cloned.1.call-done = bf16[8192,512]{1,0:T(8,128)(2,1)} async-done(((bf16[512,512]{1,0:T(8,128)(2,1)}), bf16[8192,512]{1,0:T(8,128)(2,1)}) %all-gather.7.cloned.1.call-update) | async-done | bytes 8388624 | tf_op jit(solution)/shard_map/all_gather | solution.py:24
  146.4 11.1 %convolution_convert_fusion = bf16[512,512]{1,0:T(8,128)(2,1)} fusion(bf16[512,8192]{1,0:T(8,128)(2,1)} %all-gather.5.cloned.1.call-done, bf16[8192,512]{1,0:T(8,128)(2,1)} %all-gather.7.cloned.1.call-done), kind=kOutput, calls=%fused_computation.3 | convolution fusion | flops 4295229440 | bytes 17301504 | tf_op jit(solution)/shard_map/dot_general | solution.py:22
  157.5 0.0 all-gather.9.cloned.1.call-update
  157.5 66.9 %all-gather.11.cloned.1.call-done = bf16[8192,512]{1,0:T(8,128)(2,1)} async-done(((bf16[512,512]{1,0:T(8,128)(2,1)}), bf16[8192,512]{1,0:T(8,128)(2,1)}) %all-gather.11.cloned.1.call-update) | async-done | bytes 8388624 | tf_op jit(solution)/shard_map/all_gather | solution.py:33
  224.4 57.8 %all-gather.9.cloned.1.call-done = bf16[512,8192]{1,0:T(8,128)(2,1)} async-done(((bf16[512,512]{1,0:T(8,128)(2,1)}), bf16[512,8192]{1,0:T(8,128)(2,1)}) %all-gather.9.cloned.1.call-update) | async-done | bytes 8388624 | tf_op jit(solution)/shard_map/all_gather | solution.py:29
  282.2 0.0 copy-done
  282.2 11.0 %fusion = bf16[512,512]{1,0:T(8,128)(2,1)} fusion(bf16[512,8192]{1,0:T(8,128)(2,1)} %all-gather.9.cloned.1.call-done, bf16[8192,512]{1,0:T(8,128)(2,1)} %all-gather.11.cloned.1.call-done, bf16[512,512]{1,0:T(8,128)(2,1)S(1)} %copy-done), kind=kOutput, calls=%fused_computation.2 | convolution fusion | flops 4295753728 | bytes 17825792 | tf_op jit(solution)/shard_map/dot_general | solution.py:31
  (1 shorter events, 0.0 us)
Async XLA Ops:
  6.5 63.5 %all-gather.5.cloned.1.call-start = ((), (), s32[]{:S(2)}) async-start(), calls=%async_computation | async-start | bytes 8912896 | tf_op jit(solution)/shard_map/all_gather | solution.py:14
  9.8 136.7 %all-gather.7.cloned.1.call-start = ((), (), s32[]{:S(2)}) async-start(), calls=%async_computation.1 | async-start | bytes 8912896 | tf_op jit(solution)/shard_map/all_gather | solution.py:24
  14.7 209.7 %all-gather.11.cloned.1.call-start = ((), (), s32[]{:S(2)}) async-start(), calls=%async_computation.3 | async-start | bytes 8912896 | tf_op jit(solution)/shard_map/all_gather | solution.py:33
  15.5 266.8 %copy-start = (bf16[512,512]{1,0:T(8,128)(2,1)S(1)}, bf16[512,512]{1,0:T(8,128)(2,1)}, u32[]{:S(2)}) copy-start(bf16[512,512]{1,0:T(8,128)(2,1)} %bitcast_multiply_fusion) | copy-start | bytes 1572868
  15.5 266.7 %all-gather.9.cloned.1.call-start = ((), (), s32[]{:S(2)}) async-start(), calls=%async_computation.2 | async-start | bytes 8912896 | tf_op jit(solution)/shard_map/all_gather | solution.py:29
Sparse Core Ops, SparseCore 0:
  9.9 60.1 all-gather.4
  72.5 73.8 all-gather.6
  148.9 75.4 all-gather.10
  226.1 56.0 all-gather.8
where the time goes:
time: 300 us
  waiting for transfers between devices  256 us (85%)
  matrix products  22.1 us (7%)
  between operations  13.8 us (5%)
  other arithmetic  5.36 us (2%)
    all_gather x1, waiting for transfers between devices, per_device(): lax.all_gather(sigma_tile, 'row', axis=0, tiled=True)  76.4 us
    all_gather x1, waiting for transfers between devices, per_device(): lax.all_gather(g0_tile, 'row', axis=0, tiled=True)  66.9 us
    all_gather x1, waiting for transfers between devices, per_device(): left_panel = lax.all_gather(left_tile, 'col', axis=1, tiled=True)  57.8 us
    all_gather x1, waiting for transfers between devices, per_device(): panel = lax.all_gather(g0_tile, 'col', axis=1, tiled=True)  54.6 us
    dot_general x1, matrix products, per_device(): jnp.dot(columns, lax.all_gather(sigma_tile, 'row', axis=0, tiled=True), p...  11.1 us
    dot_general x1, matrix products, per_device(): jnp.dot(columns, lax.all_gather(g0_tile, 'row', axis=0, tiled=True), pref...  11 us
  transfers between devices with their start and end apart: 4, of which 4 were waited for; matrix products, arithmetic and copies ran while one was open for 5% of the time, Pallas kernels for 0%

commit v1 on v0

--- a/solution.py
+++ b/solution.py
@@ -26,7 +26,9 @@
     )
     left_tile = left_sum.astype(jnp.bfloat16)
     start_value = g0_tile.astype(jnp.float32)
-    left_panel = lax.all_gather(left_tile, "col", axis=1, tiled=True)
+    left_panel = jnp.concatenate(
+        lax.all_to_all(jnp.stack([left_tile] * lax.axis_size("col")), "col", 0, 0), axis=1
+    )
     columns = left_panel
     result = start_value + jnp.dot(
         columns,

time: 300 us -> 370 us (1.23)
  waiting for transfers between devices: 256 us -> 315 us
  starting transfers between devices: 0.12 us -> 7.91 us
  local copies, waits for them, and re-layouts: 2.04 us -> 6.3 us
    all_to_all x0 -> x1, waiting for transfers between devices: none -> 128 us  [per_device(): lax.all_to_all(jnp.stack([left_tile] * lax.axis_size('col')), 'col', 0, 0)]
    all_gather x1 -> x0, waiting for transfers between devices: 57.8 us -> none  [per_device(): left_panel = lax.all_gather(left_tile, 'col', axis=1, tiled=True)]
    all_gather x1, waiting for transfers between devices: 66.9 us -> 55.6 us  [per_device(): lax.all_gather(g0_tile, 'row', axis=0, tiled=True)]
    all_to_all x0 -> x1, starting transfers between devices: none -> 7.83 us  [per_device(): lax.all_to_all(jnp.stack([left_tile] * lax.axis_size('col')), 'col', 0, 0)]
    another operation x0 -> x1, local copies, waits for them, and re-layouts: none -> 4.04 us  [per_device(): jnp.stack([left_tile] * lax.axis_size('col'))]
where the time goes in v1:
time: 370 us
  waiting for transfers between devices  315 us (85%)
  matrix products  21.3 us (6%)
  between operations  13.8 us (4%)
  starting transfers between devices  7.91 us (2%)
  local copies, waits for them, and re-layouts  6.3 us (2%)
  other arithmetic  5.36 us (1%)
    all_to_all x1, waiting for transfers between devices, per_device(): lax.all_to_all(jnp.stack([left_tile] * lax.axis_size('col')), 'col', 0, 0)  128 us
    all_gather x1, waiting for transfers between devices, per_device(): lax.all_gather(sigma_tile, 'row', axis=0, tiled=True)  76.4 us
    all_gather x1, waiting for transfers between devices, per_device(): lax.all_gather(g0_tile, 'row', axis=0, tiled=True)  55.6 us
    all_gather x1, waiting for transfers between devices, per_device(): panel = lax.all_gather(g0_tile, 'col', axis=1, tiled=True)  54.6 us
    dot_general x1, matrix products, per_device(): jnp.dot(columns, lax.all_gather(g0_tile, 'row', axis=0, tiled=True), pref...  11.1 us
    dot_general x1, matrix products, per_device(): jnp.dot(columns, lax.all_gather(sigma_tile, 'row', axis=0, tiled=True), p...  10.2 us
    all_to_all x1, starting transfers between devices, per_device(): lax.all_to_all(jnp.stack([left_tile] * lax.axis_size('col')), 'col', 0, 0)  7.83 us
  transfers between devices with their start and end apart: 4, of which 4 were waited for; matrix products, arithmetic and copies ran while one was open for 5% of the time, Pallas kernels for 0%

profile of v1, /device:TPU:1, one launch (start us, length us, event | category | flops | bytes accessed | tf_op | source)
XLA Modules:
  0.0 369.9 jit_solution(11557548245371235778)
XLA Ops:
  6.5 0.0 all-gather.4.cloned.1.call-start
  6.5 0.7 convert_element_type.20
  7.2 0.6 broadcast_in_dim.14
  7.9 1.9 bitcast_multiply_fusion
  9.8 0.0 all-gather.4.cloned.1.call-update
  9.8 0.0 all-gather.6.cloned.1.call-start
  10.5 0.8 fusion.4
  11.3 0.1 broadcast_in_dim.15
  11.4 2.0 scatter_fusion
  13.4 0.4 copy.6
  13.8 0.9 copy.12
  14.7 0.0 all-gather.6.cloned.1.call-update
  14.7 0.0 all-gather.8.cloned.1.call-start
  14.8 0.7 all-gather.8.cloned.1.call-update
  15.5 54.6 %all-gather.4.cloned.1.call-done = bf16[512,8192]{1,0:T(8,128)(2,1)} async-done(((bf16[512,512]{1,0:T(8,128)(2,1)}), bf16[512,8192]{1,0:T(8,128)(2,1)}) %all-gather.4.cloned.1.call-update) | async-done | bytes 8388624 | tf_op jit(solution)/shard_map/all_gather | solution.py:14
  70.1 76.4 %all-gather.6.cloned.1.call-done = bf16[8192,512]{1,0:T(8,128)(2,1)} async-done(((bf16[512,512]{1,0:T(8,128)(2,1)}), bf16[8192,512]{1,0:T(8,128)(2,1)}) %all-gather.6.cloned.1.call-update) | async-done | bytes 8388624 | tf_op jit(solution)/shard_map/all_gather | solution.py:24
  146.4 10.2 %convolution_convert_fusion = bf16[512,512]{1,0:T(8,128)(2,1)S(1)} fusion(bf16[512,8192]{1,0:T(8,128)(2,1)} %all-gather.4.cloned.1.call-done, bf16[8192,512]{1,0:T(8,128)(2,1)} %all-gather.6.cloned.1.call-done), kind=kOutput, calls=%fused_computation.3 | convolution fusion | flops 4295229440 | bytes 17301504 | tf_op jit(solution)/shard_map/dot_general | solution.py:22
  156.7 0.2 copy.7
  156.9 4.0 %stack.2 = bf16[16,512,512]{1,2,0:T(8,128)(2,1)} broadcast(bf16[512,512]{0,1:T(8,128)(2,1)S(1)} %copy.7), dimensions={1,2} | broadcast | bytes 8912896 | tf_op jit(solution)/shard_map/stack | solution.py:30
  161.0 7.8 %all-to-all-start = ((bf16[16,512,512]{1,2,0:T(8,128)(2,1)}), bf16[16,512,512]{1,2,0:T(8,128)(2,1)}, u32[]{:S(2)}, u32[]{:S(2)}) async-start(bf16[16,512,512]{1,2,0:T(8,128)(2,1)} %stack.2), calls=%async_computation | async-start | bytes 16777216 | tf_op jit(solution)/shard_map/all_to_all | solution.py:30
  168.8 55.6 %all-gather.8.cloned.1.call-done = bf16[8192,512]{1,0:T(8,128)(2,1)} async-done(((bf16[512,512]{1,0:T(8,128)(2,1)}), bf16[8192,512]{1,0:T(8,128)(2,1)}) %all-gather.8.cloned.1.call-update) | async-done | bytes 8388624 | tf_op jit(solution)/shard_map/all_gather | solution.py:35
  224.4 127.9 %all-to-all-done = bf16[16,512,512]{1,2,0:T(8,128)(2,1)} async-done(((bf16[16,512,512]{1,2,0:T(8,128)(2,1)}), bf16[16,512,512]{1,2,0:T(8,128)(2,1)}, u32[]{:S(2)}, u32[]{:S(2)}) %all-to-all-start) | async-done | bytes 8388640 | tf_op jit(solution)/shard_map/all_to_all | solution.py:30
  352.3 0.0 copy-done
  352.3 11.1 %fusion = bf16[512,512]{1,0:T(8,128)(2,1)} fusion(bf16[512,8192]{0,1:T(8,128)(2,1)} %bitcast.7, bf16[8192,512]{1,0:T(8,128)(2,1)} %all-gather.8.cloned.1.call-done, bf16[512,512]{1,0:T(8,128)(2,1)S(1)} %copy-done), kind=kOutput, calls=%fused_computation.2 | convolution fusion | flops 4295753728 | bytes 17825792 | tf_op jit(solution)/shard_map/dot_general | solution.py:33
  (2 shorter events, 0.0 us)
Async XLA Ops:
  6.5 63.5 %all-gather.4.cloned.1.call-start = ((), (), s32[]{:S(2)}) async-start(), calls=%async_computation.1 | async-start | bytes 8912896 | tf_op jit(solution)/shard_map/all_gather | solution.py:14
  9.8 136.7 %all-gather.6.cloned.1.call-start = ((), (), s32[]{:S(2)}) async-start(), calls=%async_computation.2 | async-start | bytes 8912896 | tf_op jit(solution)/shard_map/all_gather | solution.py:24
  14.7 209.7 %all-gather.8.cloned.1.call-start = ((), (), s32[]{:S(2)}) async-start(), calls=%async_computation.3 | async-start | bytes 8912896 | tf_op jit(solution)/shard_map/all_gather | solution.py:35
  160.9 191.4 %copy-start = (bf16[512,512]{1,0:T(8,128)(2,1)S(1)}, bf16[512,512]{1,0:T(8,128)(2,1)}, u32[]{:S(2)}) copy-start(bf16[512,512]{1,0:T(8,128)(2,1)} %bitcast_multiply_fusion) | copy-start | bytes 1572868
  161.0 191.4 %all-to-all-start = ((bf16[16,512,512]{1,2,0:T(8,128)(2,1)}), bf16[16,512,512]{1,2,0:T(8,128)(2,1)}, u32[]{:S(2)}, u32[]{:S(2)}) async-start(bf16[16,512,512]{1,2,0:T(8,128)(2,1)} %stack.2), calls=%async_computation | async-start | bytes 16777216 | tf_op jit(solution)/shard_map/all_to_all | solution.py:30
Sparse Core Ops, SparseCore 0:
  9.9 60.1 all-gather.3
  72.5 73.8 all-gather.5
  148.9 75.4 all-gather.7
